TPU v7x, 32 devices: a whole 2x2x4 slice. The times are simulated.
32 devices in a mesh: img: 8 (over z, y), band: 4 (over x, core).
Axes of the slice: x: 2, y: 2, z: 4, core: 2. Of those that a mesh axis runs over, the one named last changes fastest.
Arguments:
- patches: bfloat16 [32, 576, 768], P('img', 'band'), may hold values from -6 to 6
- patch_mask: int32 [32, 576], P('img', 'band'), may hold values from 0 to 1, as said below
- band_first: int32 [32, 4], P('img'), may hold values from 0 to 18, as said below
- attn_gain: bfloat16 [768], replicated, may hold values from 0.5 to 1.5
- attn_shift: bfloat16 [768], replicated, may hold values from -3 to 3
- inproj_weight: bfloat16 [768, 2304], replicated, may hold values from -0.21875 to 0.21875
- inproj_bias: bfloat16 [2304], replicated, may hold values from -2 to 2
- rotary_freqs: bfloat16 [2, 12, 32], replicated, may hold values from -3 to 3
- outproj_weight: bfloat16 [768, 768], replicated, may hold values from -0.875 to 0.875
- outproj_bias: bfloat16 [768], replicated, may hold values from -2 to 2
- mlp_gain: bfloat16 [768], replicated, may hold values from 0.5 to 1.5
- mlp_shift: bfloat16 [768], replicated, may hold values from -3 to 3
- expand_weight: bfloat16 [768, 3072], replicated, may hold values from -0.21875 to 0.21875
- expand_bias: bfloat16 [3072], replicated, may hold values from -2 to 2
- reduce_weight: bfloat16 [3072, 768], replicated, may hold values from -0.109375 to 0.109375
- reduce_bias: bfloat16 [768], replicated, may hold values from -2 to 2
- cotangent: bfloat16 [32, 576, 768], P('img', 'band'), may hold values from -6 to 6
Outputs:
- block_out: bfloat16 [32, 576, 768], P('img', 'band')
- d_patches: bfloat16 [32, 576, 768], P('img', 'band')
- grad_attn_gain: float32 [768], P('img')
- grad_attn_shift: float32 [768], P('img')
- grad_inproj_weight: float32 [768, 2304], P('img')
- grad_inproj_bias: float32 [2304], P('img')
- grad_rotary_freqs: float32 [2, 12, 32], replicated
- grad_outproj_weight: float32 [768, 768], P('img')
- grad_outproj_bias: float32 [768], P('img')
- grad_mlp_gain: float32 [768], P('img')
- grad_mlp_shift: float32 [768], P('img')
- grad_expand_weight: float32 [768, 3072], P('img')
- grad_expand_bias: float32 [3072], P('img')
- grad_reduce_weight: float32 [3072, 768], P('img')
- grad_reduce_bias: float32 [768], P('img')
Inputs may be any that keep to these rules, and one draw needn't show every extreme that they name: `patch_mask`: each image has a square grid of side 24 * 7 // 12, 20 or 24, and image 0 has side 24; the grid's rows are split over the 4 bands as evenly as possible, earlier bands taking one row more; a slot of local row i and column j of band b is 1 exactly when i is under the band's row count and j under the side. `band_first`: the first patch row of each band of each image, consistent with patch_mask's row counts.
All inputs are finite; a program needn't handle non-finite values.
Results may differ from a plain program's by a relative error of at most 0.012.
The roundings to bfloat16 on the way count: a program that leaves them out, or rounds other values in their place, can miss the bound.
Values may be sent and summed in bfloat16 or wider, within the bound.
No kernel may reach another device: no remote copies, remote signals or barrier semaphores. Data moves between devices by JAX's collectives and lax.ppermute only.
A program may use at most 192 MiB of HBM per device.

v0:
```python
import jax
import jax.numpy as jnp
from jax import lax
from jax.sharding import PartitionSpec as P

GRID = 24


EPS = 1e-06
NEG = -1e30


def layer_norm(values, gain, shift):
    center = values - jnp.mean(values, -1, keepdims=True)
    spread = jnp.mean(center * center, -1, keepdims=True)
    return center * lax.rsqrt(spread + EPS) * gain + shift


def rotate(tensor, cosine, sine):
    half_size = tensor.shape[-1] // 2
    first_half = tensor[..., :half_size]
    second_half = tensor[..., half_size:]
    return jnp.concatenate(
        [first_half * cosine - second_half * sine, first_half * sine + second_half * cosine], -1
    )


def rotate_pair(query_in, key_in, freq_in, patch_rows, patch_cols):
    angles = patch_rows[..., None, None] * freq_in[0] + patch_cols[..., None, None] * freq_in[1]
    cosine = jnp.cos(angles)
    sine = jnp.sin(angles)
    return (rotate(query_in, cosine, sine), rotate(key_in, cosine, sine))


def gelu_exact(values):
    return jax.nn.gelu(values, approximate=False)


def whole_sum(grads):
    shares = lax.psum_scatter(grads, "img", scatter_dimension=0, tiled=True)
    return lax.psum(shares, "band")


def local(
    patches,
    patch_mask,
    band_first,
    attn_gain,
    attn_shift,
    inproj_weight,
    inproj_bias,
    rotary_freqs,
    outproj_weight,
    outproj_bias,
    mlp_gain,
    mlp_shift,
    expand_weight,
    expand_bias,
    reduce_weight,
    reduce_bias,
    cotangent,
):
    single = jnp.float32
    half_type = jnp.bfloat16
    image_count, slot_count, model_width = patches.shape
    head_count = rotary_freqs.shape[1]
    head_size = model_width // head_count
    score_scale = head_size ** (-0.5)
    band_index = lax.axis_index("band")
    band_start = lax.dynamic_index_in_dim(band_first, band_index, 1, keepdims=False)
    slot_index = jnp.arange(slot_count)
    patch_rows = (band_start[:, None] + (slot_index // GRID)[None, :]).astype(single)
    patch_cols = jnp.broadcast_to((slot_index % GRID).astype(single)[None, :], patch_rows.shape)
    real_slot = patch_mask.astype(single)
    key_flag = patch_mask.astype(half_type)
    patches_wide = patches.astype(single)
    normed_one, pull_first = jax.vjp(
        layer_norm, patches_wide, attn_gain.astype(single), attn_shift.astype(single)
    )
    attn_in = normed_one.astype(half_type)
    projected = jnp.dot(attn_in, inproj_weight, preferred_element_type=single) + inproj_bias.astype(
        single
    )
    shape_heads = (image_count, slot_count, head_count, head_size)
    queries = projected[..., :model_width].reshape(shape_heads)
    keys_own = projected[..., model_width : 2 * model_width].reshape(shape_heads)
    values_own = projected[..., 2 * model_width :].reshape(shape_heads)
    (query_turned, key_turned), pull_turn = jax.vjp(
        lambda query_in, key_in, freq_in: rotate_pair(
            query_in, key_in, freq_in, patch_rows, patch_cols
        ),
        queries,
        keys_own,
        rotary_freqs.astype(single),
    )
    query_rot = query_turned.astype(half_type)
    key_rot = key_turned.astype(half_type)
    value_low = values_own.astype(half_type)
    keys_all, values_all, flags_all = (
        lax.all_gather(key_rot, "band", axis=1, tiled=True),
        lax.all_gather(value_low, "band", axis=1, tiled=True),
        lax.all_gather(key_flag, "band", axis=1, tiled=True),
    )
    scores = (
        jnp.einsum("iqhd,ikhd->ihqk", query_rot, keys_all, preferred_element_type=single)
        * score_scale
    )
    masked = jnp.where(flags_all[:, None, None, :] > 0, scores, NEG)
    row_max = jnp.max(masked, -1, keepdims=True)
    expo = jnp.exp(masked - row_max)
    row_total = jnp.sum(expo, -1, keepdims=True)
    soft_probs = expo / row_total
    log_total = row_max + jnp.log(row_total)
    probs_low = soft_probs.astype(half_type)
    attn_mix = jnp.einsum("ihqk,ikhd->iqhd", probs_low, values_all, preferred_element_type=single)
    attn_mix = attn_mix.reshape(image_count, slot_count, model_width).astype(half_type)
    attn_out = jnp.dot(
        attn_mix, outproj_weight, preferred_element_type=single
    ) + outproj_bias.astype(single)
    resid_mid = patches_wide + attn_out
    normed_two, pull_second = jax.vjp(
        layer_norm, resid_mid, mlp_gain.astype(single), mlp_shift.astype(single)
    )
    mlp_in = normed_two.astype(half_type)
    pre_act = jnp.dot(mlp_in, expand_weight, preferred_element_type=single) + expand_bias.astype(
        single
    )
    hidden_act, pull_gelu = jax.vjp(gelu_exact, pre_act)
    hidden = hidden_act.astype(half_type)
    branch = jnp.dot(hidden, reduce_weight, preferred_element_type=single) + reduce_bias.astype(
        single
    )
    block_out = (real_slot[..., None] * (resid_mid + branch)).astype(half_type)
    grad_top = cotangent.astype(single) * real_slot[..., None]
    grad_low = grad_top.astype(half_type)
    grad_reduce_weight = jnp.einsum("iqf,iqd->fd", hidden, grad_low, preferred_element_type=single)
    grad_reduce_bias = jnp.sum(grad_low.astype(single), (0, 1))
    d_hidden = jnp.einsum("iqd,fd->iqf", grad_low, reduce_weight, preferred_element_type=single)
    (d_pre_wide,) = pull_gelu(d_hidden)
    d_pre = d_pre_wide.astype(half_type)
    grad_expand_weight = jnp.einsum("iqd,iqf->df", mlp_in, d_pre, preferred_element_type=single)
    grad_expand_bias = jnp.sum(d_pre.astype(single), (0, 1))
    d_mlp_in = jnp.einsum("iqf,df->iqd", d_pre, expand_weight, preferred_element_type=single)
    d_mid_norm, grad_mlp_gain, grad_mlp_shift = pull_second(d_mlp_in)
    d_mid = grad_top + d_mid_norm
    mlp_grads = (
        grad_mlp_gain,
        grad_mlp_shift,
        grad_expand_weight,
        grad_expand_bias,
        grad_reduce_weight,
        grad_reduce_bias,
    )
    d_attn = d_mid.astype(half_type)
    grad_outproj_weight = jnp.einsum("iqe,iqd->ed", attn_mix, d_attn, preferred_element_type=single)
    grad_outproj_bias = jnp.sum(d_attn.astype(single), (0, 1))
    d_mix = jnp.einsum("iqd,ed->iqe", d_attn, outproj_weight, preferred_element_type=single)
    d_mix = d_mix.astype(half_type).reshape(shape_heads)
    keys_back, values_back, flags_back = (
        lax.all_gather(key_rot, "band", axis=1, tiled=True),
        lax.all_gather(value_low, "band", axis=1, tiled=True),
        lax.all_gather(key_flag, "band", axis=1, tiled=True),
    )
    scores_again = (
        jnp.einsum("iqhd,ikhd->ihqk", query_rot, keys_back, preferred_element_type=single)
        * score_scale
    )
    masked_again = jnp.where(flags_back[:, None, None, :] > 0, scores_again, NEG)
    probs_again = jnp.exp(masked_again - log_total)
    probs_round = probs_again.astype(half_type)
    d_values = jnp.einsum("ihqk,iqhd->ikhd", probs_round, d_mix, preferred_element_type=single)
    d_probs = jnp.einsum("iqhd,ikhd->ihqk", d_mix, values_back, preferred_element_type=single)
    row_inner = jnp.sum(probs_again * d_probs, -1, keepdims=True)
    d_scores = (probs_again * (d_probs - row_inner)).astype(half_type)
    d_qrot = (
        jnp.einsum("ihqk,ikhd->iqhd", d_scores, keys_back, preferred_element_type=single)
        * score_scale
    )
    d_krot_all = (
        jnp.einsum("ihqk,iqhd->ikhd", d_scores, query_rot, preferred_element_type=single)
        * score_scale
    )
    d_krot, d_vals_own = (
        lax.psum_scatter(d_krot_all, "band", scatter_dimension=1, tiled=True),
        lax.psum_scatter(d_values, "band", scatter_dimension=1, tiled=True),
    )
    d_queries, d_keys, grad_rotary_freqs = pull_turn((d_qrot, d_krot))
    flat_shape = (image_count, slot_count, model_width)
    d_proj = jnp.concatenate(
        [d_queries.reshape(flat_shape), d_keys.reshape(flat_shape), d_vals_own.reshape(flat_shape)],
        -1,
    ).astype(half_type)
    grad_inproj_weight = jnp.einsum("iqd,iqe->de", attn_in, d_proj, preferred_element_type=single)
    grad_inproj_bias = jnp.sum(d_proj.astype(single), (0, 1))
    d_attn_in = jnp.einsum("iqe,de->iqd", d_proj, inproj_weight, preferred_element_type=single)
    d_norm, grad_attn_gain, grad_attn_shift = pull_first(d_attn_in)
    d_patches = (d_mid + d_norm).astype(half_type)
    freq_total = lax.psum(grad_rotary_freqs, ("img", "band"))
    every_sum = whole_sum(
        (
            grad_attn_gain,
            grad_attn_shift,
            grad_inproj_weight,
            grad_inproj_bias,
            grad_outproj_weight,
            grad_outproj_bias,
        )
        + mlp_grads
    )
    attn_sums = every_sum[:6]
    mlp_sums = every_sum[6:]
    return (
        block_out,
        d_patches,
        attn_sums[0],
        attn_sums[1],
        attn_sums[2],
        attn_sums[3],
        freq_total,
        attn_sums[4],
        attn_sums[5],
        mlp_sums[0],
        mlp_sums[1],
        mlp_sums[2],
        mlp_sums[3],
        mlp_sums[4],
        mlp_sums[5],
    )


def solution(mesh):
    return jax.shard_map(
        local,
        mesh=mesh,
        in_specs=(
            P("img", "band", None),
            P("img", "band"),
            P("img", None),
            P(),
            P(),
            P(),
            P(),
            P(),
            P(),
            P(),
            P(),
            P(),
            P(),
            P(),
            P(),
            P(),
            P("img", "band", None),
        ),
        out_specs=(
            P("img", "band", None),
            P("img", "band", None),
            P("img"),
            P("img"),
            P("img", None),
            P("img"),
            P(),
            P("img", None),
            P("img"),
            P("img"),
            P("img"),
            P("img", None),
            P("img"),
            P("img", None),
            P("img"),
        ),
        check_vma=False,
    )
```

profile of v0, /device:TPU:0, one launch (start us, length us, event | category | flops | bytes accessed | tf_op | source)
XLA Modules:
  0.0 1027.3 jit_solution(12210744125189027709)
XLA Ops:
  29.4 10.2 subtract_convert_fusion.1
  64.5 34.6 %all-gather.6.cloned.1.call-done = bf16[4,576,12,64]{3,0,2,1:T(4,128)(2,1)} async-done(((bf16[4,144,12,64]{3,0,2,1:T(4,128)(2,1)}), bf16[4,576,12,64]{3,0,2,1:T(4,128)(2,1)}) %all-gather.6.cloned.1.call-update) | async-done | bytes 3538960 | tf_op jit(solution)/shard_map/all_gather | solution.py:100
  99.1 10.5 %copy.81 = bf16[4,576,12,64]{1,3,2,0:T(8,128)(2,1)} copy(bf16[4,576,12,64]{3,0,2,1:T(4,128)(2,1)} %all-gather.6.cloned.1.call-done) | data formatting | bytes 7077888 | tf_op jit(solution)/shard_map/all_gather | solution.py:100
  109.6 7.7 fusion.6
  125.0 26.5 %all-gather.4.cloned.1.call-done = bf16[4,576,12,64]{3,0,2,1:T(4,128)(2,1)} async-done(((bf16[4,144,12,64]{3,0,2,1:T(4,128)(2,1)}), bf16[4,576,12,64]{3,0,2,1:T(4,128)(2,1)}) %all-gather.4.cloned.1.call-update) | async-done | bytes 3538960 | tf_op jit(solution)/shard_map/all_gather | solution.py:101
  151.5 10.4 %copy.82 = bf16[4,576,12,64]{1,3,2,0:T(8,128)(2,1)} copy(bf16[4,576,12,64]{3,0,2,1:T(4,128)(2,1)} %all-gather.4.cloned.1.call-done) | data formatting | bytes 7077888 | tf_op jit(solution)/shard_map/all_gather | solution.py:101
  161.9 10.1 fusion.43
  173.6 7.5 fusion.42
  181.1 17.0 %multiply_convert_fusion.1 = (bf16[4,144,3072]{2,1,0:T(8,128)(2,1)}, f32[4,144,3072]{2,1,0:T(8,128)S(1)}) fusion(f32[4,144,3072]{2,1,0:T(8,128)S(1)} %get-tuple-element.121, f32[3072]{0:T(1024)S(1)} %copy-done.31, u8[144,3072]{1,0:T(8,128)(4,1)S(1)} %get-tuple-element.61, u8[144,3072]{1,0:T(8,128)(4,1)S(1)} %get-tuple-element.60), kind=kLoop, calls=%fused_computation.22 | loop fusion | flops 125632512 | bytes 18591744 | tf_op jit(solution)/shard_map/convert_element_type | solution.py:129
  198.2 8.5 convert_reduce_fusion
  206.7 7.6 multiply_reduce_fusion.1
  222.5 10.6 %fusion.24 = f32[4,576,12,64]{1,3,2,0:T(8,128)} fusion(bf16[4,144,12,64]{1,3,2,0:T(8,128)(2,1)} %bitcast.101, f32[4,12,144]{2,1,0:T(8,128)} %log_add_fusion, f32[4,12,144,576]{3,2,1,0:T(8,128)} %copy-done.1, pred[4,576]{1,0:T(4,128)(4,1)S(1)} %bitcast.111), kind=kOutput, calls=%fused_computation.54 | convolution fusion | flops 525533184 | bytes 23917824 | tf_op jit(solution)/shard_map/ihqk,iqhd->ikhd/dot_general | solution.py:171
  233.2 18.3 %copy.96 = f32[4,576,12,64]{3,2,0,1:T(8,128)} copy(f32[4,576,12,64]{1,3,2,0:T(8,128)} %fusion.24) | data formatting | bytes 14155776
  251.5 14.7 %reshape.210 = f32[576,3072]{1,0:T(8,128)} reshape(f32[576,4,12,64]{3,2,1,0:T(8,128)} %bitcast.94) | data formatting | bytes 14155776
  266.3 17.1 %multiply_reduce_fusion = (f32[4,12,144]{2,1,0:T(8,128)S(1)}, f32[4,12,144,576]{3,2,1,0:T(8,128)}) fusion(f32[4,12,144]{2,1,0:T(8,128)} %log_add_fusion, f32[4,12,144,576]{3,2,1,0:T(8,128)} %copy-done.1, pred[4,576]{1,0:T(4,128)(4,1)S(1)} %bitcast.112, bf16[4,144,12,64]{1,3,2,0:T(8,128)(2,1)} %bitcast.102, bf16[4,576,12,64]{1,3,2,0:T(8,128)(2,1)} %copy.82), kind=kOutput, calls=%fused_computation.1 | convolution fusion | flops 529507584 | bytes 36331776 | tf_op jit(solution)/shard_map/iqhd,ikhd->ihqk/dot_general | solution.py:172
  283.4 14.2 %multiply_convert_fusion = bf16[4,12,144,576]{3,2,1,0:T(8,128)(2,1)S(1)} fusion(f32[4,12,144,576]{3,2,1,0:T(8,128)} %get-tuple-element.124, f32[4,12,144]{2,1,0:T(8,128)S(1)} %get-tuple-element.123, f32[4,12,144]{2,1,0:T(8,128)S(1)} %copy-done.16, f32[4,12,144,576]{3,2,1,0:T(8,128)} %copy-done.1, pred[4,576]{1,0:T(4,128)(4,1)S(1)} %bitcast.113), kind=kLoop, calls=%fused_computation | loop fusion | flops 23887872 | bytes 39870720 | tf_op jit(solution)/shard_map/convert_element_type | solution.py:174
  305.1 18.3 %copy.94 = f32[4,576,12,64]{3,2,0,1:T(8,128)} copy(f32[4,576,12,64]{1,3,2,0:T(8,128)} %multiply_bitcast_fusion) | data formatting | bytes 14155776
  323.5 14.7 %reshape.208 = f32[576,3072]{1,0:T(8,128)} reshape(f32[576,4,12,64]{3,2,1,0:T(8,128)} %bitcast.95) | data formatting | bytes 14155776
  342.6 11.5 %convolution_bitcast_fusion.1 = f32[768,3072]{1,0:T(8,128)} fusion(bf16[4,144,3072]{2,1,0:T(8,128)(2,1)} %copy-done.12, f32[4,144,768]{2,1,0:T(8,128)} %copy-done.3, f32[768]{0:T(1024)S(1)} %copy-done.21, f32[768]{0:T(1024)S(1)} %convert_element_type.131, f32[4,144]{1,0:T(4,128)S(1)} %fusion.58, f32[4,144]{1,0:T(4,128)S(1)} %broadcast_multiply_fusion), kind=kOutput, calls=%fused_computation.36 | convolution fusion | flops 2720120832 | bytes 14756352 | tf_op jit(solution)/shard_map/iqd,iqf->df/dot_general | solution.py:141
  354.7 9.8 convolution_bitcast_fusion
  364.6 10.0 multiply_bitcast_fusion.1
  386.0 16.4 %reduce-scatter.19.cloned.1.call-done = f32[144,3072]{1,0:T(8,128)} async-done(((f32[576,3072]{1,0:T(8,128)}), f32[144,3072]{1,0:T(8,128)}) %reduce-scatter.19.cloned.1.call-update) | async-done | bytes 1769488
  407.1 8.8 fusion.73
  426.7 11.9 %multiply_add_fusion = (f32[4,144,12,32]{1,3,2,0:T(8,128)}, f32[4,144,12,32]{1,3,2,0:T(8,128)S(1)}, f32[4,144,12,32]{1,3,2,0:T(8,128)S(1)}, f32[4,144,12,32]{1,3,2,0:T(8,128)S(1)}, f32[4,144,12,32]{1,3,2,0:T(8,128)S(1)}) fusion(f32[4,144,12,32]{1,3,2,0:T(8,128)} %copy.99, f32[4,144,12,32]{1,3,2,0:T(8,128)} %copy.98, ...), kind=kLoop, calls=%fused_computation.92 | loop fusion | flops 7741440 | bytes 11507520 | tf_op jit(solution)/shard_map/transpose(jvp())/add_any | solution.py:30
  445.6 8.1 convolution_bitcast_fusion.2
  456.9 8.0 multiply_convert_fusion.2
  465.9 40.5 %psum.95 = f32[2,12,32]{2,1,0:T(8,128)S(1)} all-reduce(f32[2,12,32]{2,1,0:T(8,128)} %pad_add_fusion), channel_id=1, replica_groups=mesh['img'=8,'band'=4] {'img','band'}, use_global_device_ids=true, to_apply=%region_26.27 | all-reduce | flops 768 | bytes 6144 | tf_op jit(solution)/shard_map/psum | solution.py:198
  509.2 131.7 %reduce-scatter.15.cloned.1.call-done = f32[96,3072]{1,0:T(8,128)} async-done(((f32[768,3072]{1,0:T(8,128)}), f32[96,3072]{1,0:T(8,128)}) %reduce-scatter.15.cloned.1.call-update) | async-done | bytes 1179664 | tf_op jit(solution)/shard_map/reduce_scatter | solution.py:40
  640.9 164.8 %reduce-scatter.17.cloned.1.call-done = f32[384,768]{1,0:T(8,128)} async-done(((f32[3072,768]{1,0:T(8,128)}), f32[384,768]{1,0:T(8,128)}) %reduce-scatter.17.cloned.1.call-update) | async-done | bytes 1179664 | tf_op jit(solution)/shard_map/reduce_scatter | solution.py:40
  805.7 131.9 %reduce-scatter.11.cloned.1.call-done = f32[96,2304]{1,0:T(8,128)} async-done(((f32[768,2304]{1,0:T(8,128)}), f32[96,2304]{1,0:T(8,128)}) %reduce-scatter.11.cloned.1.call-update) | async-done | bytes 884752 | tf_op jit(solution)/shard_map/reduce_scatter | solution.py:40
  944.4 36.9 %all-reduce.14 = (f32[768]{0:T(1024)}, f32[768]{0:T(1024)}, f32[2304]{0:T(1024)}, f32[768]{0:T(1024)}, f32[768]{0:T(1024)}, /*index=5*/f32[768]{0:T(1024)}, f32[3072]{0:T(1024)}, f32[768]{0:T(1024)}) all-reduce(f32[768]{0:T(1024)} %get-tuple-element.64, f32[768]{0:T(1024)} %get-tuple-element.67, ...), channel_id=4, replica_groups=mesh['img'=8,'band'=4] {'img'}, use_global_device_ids=true, to_apply=%region_14.15.clone | all-reduce | flops 9984 | bytes 79872
  1001.9 12.7 %all-reduce.19.cloned.1.call-done = (f32[96,2304]{1,0:T(8,128)}, f32[96,768]{1,0:T(8,128)}, f32[96,3072]{1,0:T(8,128)}, f32[384,768]{1,0:T(8,128)}) async-done(((f32[96,2304]{1,0:T(8,128)}, f32[96,768]{1,0:T(8,128)}, f32[96,3072]{1,0:T(8,128)}, f32[384,768]{1,0:T(8,128)}), (f32[96,2304]{1,0:T(8,128)}, f32[96,768]{1,0:T(8,128)}, f32[96,3072]{1,0:T(8,128)}, ...) | async-done | bytes 3538960 | tf_op jit(solution)/shard_map/psum | solution.py:41
  (210 shorter events, 149.0 us)
Async XLA Ops:
  7.2 7.0 copy-start
  7.2 91.9 %all-gather.6.cloned.1.call-start = ((), (), s32[]{:S(2)}) async-start(), calls=%async_computation.7 | async-start | bytes 8847360 | tf_op jit(solution)/shard_map/all_gather | solution.py:100
  9.1 5.1 copy-start.35
  14.2 15.1 %copy-start.22 = (f32[12,32]{1,0:T(8,128)}, f32[12,32]{1,0:T(8,128)S(1)}, u32[]{:S(2)}) copy-start(f32[12,32]{1,0:T(8,128)S(1)} %get-tuple-element.113) | copy-start | bytes 4612
  14.2 15.1 %copy-start.24 = (f32[12,32]{1,0:T(8,128)}, f32[12,32]{1,0:T(8,128)S(1)}, u32[]{:S(2)}) copy-start(f32[12,32]{1,0:T(8,128)S(1)} %get-tuple-element.114) | copy-start | bytes 4612
  29.4 10.2 copy-start.26
  45.3 106.2 %all-gather.4.cloned.1.call-start = ((), (), s32[]{:S(2)}) async-start(), calls=%async_computation.6 | async-start | bytes 8847360 | tf_op jit(solution)/shard_map/all_gather | solution.py:101
  50.4 5.6 copy-start.48
  54.6 320.0 %reduce-scatter.21.cloned.1.call-start = ((), (), s32[]{:S(2)}) async-start(), calls=%async_computation.13 | async-start | bytes 8847360
  117.3 6.1 copy-start.1
  117.3 6.4 copy-start.18
  161.9 10.1 copy-start.5
  161.9 10.1 copy-start.52
  173.2 41.2 %copy-start.3 = (f32[4,144,768]{2,1,0:T(8,128)}, f32[4,144,768]{2,1,0:T(8,128)S(1)}, u32[]{:S(2)}) copy-start(f32[4,144,768]{2,1,0:T(8,128)S(1)} %get-tuple-element.120) | copy-start | bytes 5308420
  181.1 17.1 %copy-start.13 = (bf16[4,144,768]{2,1,0:T(8,128)(2,1)S(1)}, bf16[4,144,768]{2,1,0:T(8,128)(2,1)}, u32[]{:S(2)}) copy-start(bf16[4,144,768]{2,1,0:T(8,128)(2,1)} %param.33) | copy-start | bytes 2654212
  181.1 17.1 %copy-start.41 = (f32[4,144]{1,0:T(4,128)S(1)}, f32[4,144]{1,0:T(4,128)}, u32[]{:S(2)}) copy-start(f32[4,144]{1,0:T(4,128)} %get-tuple-element.115) | copy-start | bytes 6916
  206.7 7.6 copy-start.12
  266.2 136.2 %reduce-scatter.19.cloned.1.call-start = ((), (), s32[]{:S(2)}) async-start(), calls=%async_computation.12 | async-start | bytes 8847360
  266.3 17.1 %copy-start.16 = (f32[4,12,144]{2,1,0:T(8,128)S(1)}, f32[4,12,144]{2,1,0:T(8,128)}, u32[]{:S(2)}) copy-start(f32[4,12,144]{2,1,0:T(8,128)} %log_add_fusion) | copy-start | bytes 82948
  283.4 17.7 %copy-start.7 = (bf16[4,144,12,32]{1,3,2,0:T(8,128)(2,1)S(1)}, bf16[4,144,12,32]{1,3,2,0:T(8,128)(2,1)}, u32[]{:S(2)}) copy-start(bf16[4,144,12,32]{1,3,2,0:T(8,128)(2,1)} %get-tuple-element.106) | copy-start | bytes 1327108
  283.4 17.7 %copy-start.8 = (bf16[4,144,12,32]{1,3,2,0:T(8,128)(2,1)S(1)}, bf16[4,144,12,32]{1,3,2,0:T(8,128)(2,1)}, u32[]{:S(2)}) copy-start(bf16[4,144,12,32]{1,3,2,0:T(8,128)(2,1)} %get-tuple-element.107) | copy-start | bytes 1327108
  338.2 170.9 %reduce-scatter.13.cloned.1.call-start = ((), (), s32[]{:S(2)}) async-start(), calls=%async_computation.9 | async-start | bytes 2654208 | tf_op jit(solution)/shard_map/reduce_scatter | solution.py:40
  342.5 298.4 %reduce-scatter.15.cloned.1.call-start = ((), (), s32[]{:S(2)}) async-start(), calls=%async_computation.10 | async-start | bytes 10616832 | tf_op jit(solution)/shard_map/reduce_scatter | solution.py:40
  354.1 451.7 %reduce-scatter.17.cloned.1.call-start = ((), (), s32[]{:S(2)}) async-start(), calls=%async_computation.11 | async-start | bytes 10616832 | tf_op jit(solution)/shard_map/reduce_scatter | solution.py:40
  364.6 573.1 %reduce-scatter.11.cloned.1.call-start = ((), (), s32[]{:S(2)}) async-start(), calls=%async_computation.8 | async-start | bytes 7962624 | tf_op jit(solution)/shard_map/reduce_scatter | solution.py:40
  421.3 5.4 copy-start.23
  421.3 5.4 copy-start.25
  453.7 561.0 %all-reduce.19.cloned.1.call-start = ((), (), s32[]{:S(2)}) async-start(), calls=%async_computation.14 | async-start | bytes 7077888 | tf_op jit(solution)/shard_map/psum | solution.py:41
  456.8 8.1 copy-start.10
  456.8 8.1 copy-start.27
  456.9 8.0 copy-start.45
  507.0 430.7 %copy-start.30 = (f32[4,144]{1,0:T(4,128)S(1)}, f32[4,144]{1,0:T(4,128)}, u32[]{:S(2)}) copy-start(f32[4,144]{1,0:T(4,128)} %copy-done.28) | copy-start | bytes 6916
  (33 other events, 103.3 us)
Sparse Core Ops, SparseCore 0:
  45.5 53.5 all-gather.5
  100.6 50.8 all-gather.3
  266.4 64.1 reduce-scatter.20
  338.3 64.0 reduce-scatter.18
  405.8 69.6 reduce-scatter.12
  478.9 161.9 reduce-scatter.14
  644.5 161.2 reduce-scatter.16
  809.4 128.2 reduce-scatter.10
  940.3 74.2 all-reduce.18
where the time goes:
time: 1040 us; the launch traced here: 1030 us
  waiting for transfers between devices  519 us (50%)
  local copies, waits for them, and re-layouts  178 us (17%)
  matrix products  136 us (13%)
  blocking collectives  91.4 us (9%)
  other arithmetic  84.9 us (8%)
  between operations  16.6 us (2%)
    reduce_scatter x4, waiting for transfers between devices, whole_sum(): shares = lax.psum_scatter(grads, 'img', scatter_dimension=0, tiled=True)  428 us
    unnamed x135, local copies, waits for them, and re-layouts  116 us
    psum x1, blocking collectives, local(): freq_total = lax.psum(grad_rotary_freqs, ('img', 'band'))  40.5 us
    unnamed x1, blocking collectives  36.9 us
    all_gather x1, waiting for transfers between devices, local(): lax.all_gather(key_rot, 'band', axis=1, tiled=True)  34.6 us
    all_gather x1, waiting for transfers between devices, local(): lax.all_gather(value_low, 'band', axis=1, tiled=True)  26.5 us
  transfers between devices with their start and end apart: 9, of which 7 were waited for; matrix products, arithmetic and copies ran while one was open for 23% of the time, Pallas kernels for 0%

commit v1 on v0

v1 whole, which is shorter than its diff:
```python
import jax
import jax.numpy as jnp
from jax import lax
from jax.sharding import PartitionSpec as P

GRID = 24
EPS = 1e-06
NEG = -1e30


def norm_parts(values):
    center = values - jnp.mean(values, -1, keepdims=True)
    rstd = lax.rsqrt(jnp.mean(center * center, -1, keepdims=True) + EPS)
    return center * rstd, rstd


def norm_back(grad, gain, xhat, rstd):
    scaled = grad * gain
    inner = jnp.mean(scaled * xhat, -1, keepdims=True)
    return rstd * (scaled - jnp.mean(scaled, -1, keepdims=True) - xhat * inner)


def turn(tensor, cosine, sine):
    half = tensor.shape[-1] // 2
    first, second = tensor[..., :half], tensor[..., half:]
    return jnp.concatenate(
        [first * cosine - second * sine, first * sine + second * cosine], -1
    )


def matrix_sum(grad):
    low = grad.astype(jnp.bfloat16)
    low = lax.psum_scatter(low, "band", scatter_dimension=1, tiled=True)
    low = lax.psum_scatter(low, "img", scatter_dimension=0, tiled=True)
    low = lax.all_gather(low, "band", axis=1, tiled=True)
    return low.astype(jnp.float32)


def local(
    patches,
    patch_mask,
    band_first,
    attn_gain,
    attn_shift,
    inproj_weight,
    inproj_bias,
    rotary_freqs,
    outproj_weight,
    outproj_bias,
    mlp_gain,
    mlp_shift,
    expand_weight,
    expand_bias,
    reduce_weight,
    reduce_bias,
    cotangent,
):
    single = jnp.float32
    low = jnp.bfloat16
    images, slots, width = patches.shape
    heads = rotary_freqs.shape[1]
    size = width // heads
    scale = size ** (-0.5)
    bands = lax.axis_size("band")
    here = lax.axis_index("band")

    def gather_image(values):
        return lax.all_to_all(values, "band", 0, 1, tiled=True)

    def spread_image(values):
        return lax.all_to_all(values, "band", 1, 0, tiled=True)

    patches = gather_image(patches)
    cotangent = gather_image(cotangent)
    mask = gather_image(patch_mask).astype(single)
    count = images // bands
    total = slots * bands
    starts = lax.dynamic_slice_in_dim(band_first, here * count, count, 0)
    row_in = jnp.arange(slots) // GRID
    rows = (starts[:, :, None] + row_in[None, None, :]).reshape(count, total).astype(single)
    cols = jnp.broadcast_to(
        (jnp.arange(total) % GRID).astype(single)[None, :], rows.shape
    )
    freqs = rotary_freqs.astype(single)
    angles = rows[..., None, None] * freqs[0] + cols[..., None, None] * freqs[1]
    cosine, sine = jnp.cos(angles), jnp.sin(angles)

    wide = patches.astype(single)
    xhat_one, rstd_one = norm_parts(wide)
    gain_one = attn_gain.astype(single)
    attn_in = (xhat_one * gain_one + attn_shift.astype(single)).astype(low)
    projected = jnp.dot(attn_in, inproj_weight, preferred_element_type=single)
    projected = projected + inproj_bias.astype(single)
    split = projected.reshape(count, total, 3, heads, size)
    query_rot = turn(split[:, :, 0], cosine, sine).astype(low)
    key_rot = turn(split[:, :, 1], cosine, sine).astype(low)
    value_low = split[:, :, 2].astype(low)
    scores = jnp.einsum("iqhd,ikhd->ihqk", query_rot, key_rot, preferred_element_type=single)
    masked = jnp.where(mask[:, None, None, :] > 0, scores * scale, NEG)
    expo = jnp.exp(masked - jnp.max(masked, -1, keepdims=True))
    probs = expo / jnp.sum(expo, -1, keepdims=True)
    probs_low = probs.astype(low)
    mix = jnp.einsum("ihqk,ikhd->iqhd", probs_low, value_low, preferred_element_type=single)
    mix = mix.reshape(count, total, width).astype(low)
    attn_out = jnp.dot(mix, outproj_weight, preferred_element_type=single)
    resid_mid = wide + attn_out + outproj_bias.astype(single)
    xhat_two, rstd_two = norm_parts(resid_mid)
    gain_two = mlp_gain.astype(single)
    mlp_in = (xhat_two * gain_two + mlp_shift.astype(single)).astype(low)
    pre_act = jnp.dot(mlp_in, expand_weight, preferred_element_type=single)
    pre_act = pre_act + expand_bias.astype(single)
    half_erf = 0.5 + 0.5 * lax.erf(pre_act * (0.5**0.5))
    hidden = (pre_act * half_erf).astype(low)
    slope = half_erf + pre_act * jnp.exp(-0.5 * pre_act * pre_act) * 0.3989422804014327
    branch = jnp.dot(hidden, reduce_weight, preferred_element_type=single)
    block_out = mask[..., None] * (resid_mid + branch + reduce_bias.astype(single))
    block_out = spread_image(block_out.astype(low))

    grad_top = cotangent.astype(single) * mask[..., None]
    grad_low = grad_top.astype(low)
    grad_reduce_weight = jnp.einsum("iqf,iqd->fd", hidden, grad_low, preferred_element_type=single)
    grad_reduce_bias = jnp.sum(grad_top, (0, 1))
    d_hidden = jnp.einsum("iqd,fd->iqf", grad_low, reduce_weight, preferred_element_type=single)
    d_pre = (d_hidden * slope).astype(low)
    grad_expand_weight = jnp.einsum("iqd,iqf->df", mlp_in, d_pre, preferred_element_type=single)
    grad_expand_bias = jnp.sum(d_pre.astype(single), (0, 1))
    d_mlp_in = jnp.einsum("iqf,df->iqd", d_pre, expand_weight, preferred_element_type=single)
    grad_mlp_gain = jnp.sum(d_mlp_in * xhat_two, (0, 1))
    grad_mlp_shift = jnp.sum(d_mlp_in, (0, 1))
    d_mid = grad_top + norm_back(d_mlp_in, gain_two, xhat_two, rstd_two)
    d_attn = d_mid.astype(low)
    grad_outproj_weight = jnp.einsum("iqe,iqd->ed", mix, d_attn, preferred_element_type=single)
    grad_outproj_bias = jnp.sum(d_attn.astype(single), (0, 1))
    d_mix = jnp.einsum("iqd,ed->iqe", d_attn, outproj_weight, preferred_element_type=single)
    d_mix = d_mix.astype(low).reshape(count, total, heads, size)
    d_values = jnp.einsum("ihqk,iqhd->ikhd", probs_low, d_mix, preferred_element_type=single)
    d_probs = jnp.einsum("iqhd,ikhd->ihqk", d_mix, value_low, preferred_element_type=single)
    inner = jnp.sum(probs * d_probs, -1, keepdims=True)
    d_scores = (probs * (d_probs - inner)).astype(low)
    d_qrot = scale * jnp.einsum("ihqk,ikhd->iqhd", d_scores, key_rot, preferred_element_type=single)
    d_krot = scale * jnp.einsum("ihqk,iqhd->ikhd", d_scores, query_rot, preferred_element_type=single)
    half = size // 2
    slope_q = d_qrot[..., half:] * query_rot[..., :half] - d_qrot[..., :half] * query_rot[..., half:]
    slope_k = d_krot[..., half:] * key_rot[..., :half] - d_krot[..., :half] * key_rot[..., half:]
    d_angle = slope_q + slope_k
    grad_freqs = jnp.stack(
        [
            jnp.sum(rows[..., None, None] * d_angle, (0, 1)),
            jnp.sum(cols[..., None, None] * d_angle, (0, 1)),
        ]
    )
    d_queries = turn(d_qrot, cosine, -sine)
    d_keys = turn(d_krot, cosine, -sine)
    flat = (count, total, width)
    d_proj = jnp.concatenate(
        [d_queries.reshape(flat), d_keys.reshape(flat), d_values.reshape(flat)], -1
    ).astype(low)
    grad_inproj_weight = jnp.einsum("iqd,iqe->de", attn_in, d_proj, preferred_element_type=single)
    grad_inproj_bias = jnp.sum(d_proj.astype(single), (0, 1))
    d_attn_in = jnp.einsum("iqe,de->iqd", d_proj, inproj_weight, preferred_element_type=single)
    grad_attn_gain = jnp.sum(d_attn_in * xhat_one, (0, 1))
    grad_attn_shift = jnp.sum(d_attn_in, (0, 1))
    d_patches = d_mid + norm_back(d_attn_in, gain_one, xhat_one, rstd_one)
    d_patches = spread_image(d_patches.astype(low))

    small = (
        grad_attn_gain,
        grad_attn_shift,
        grad_inproj_bias,
        grad_outproj_bias,
        grad_mlp_gain,
        grad_mlp_shift,
        grad_expand_bias,
        grad_reduce_bias,
        grad_freqs.reshape(-1),
    )
    packed = lax.psum(jnp.concatenate(small), ("img", "band"))
    shares = lax.axis_size("img")
    mine = lax.axis_index("img")
    sums = []
    at = 0
    for piece in small:
        long = piece.shape[0]
        sums.append(packed[at : at + long])
        at += long
    freq_total = sums.pop().reshape(grad_freqs.shape)
    sums = [
        lax.dynamic_slice_in_dim(s, mine * (s.shape[0] // shares), s.shape[0] // shares)
        for s in sums
    ]
    return (
        block_out,
        d_patches,
        sums[0],
        sums[1],
        matrix_sum(grad_inproj_weight),
        sums[2],
        freq_total,
        matrix_sum(grad_outproj_weight),
        sums[3],
        sums[4],
        sums[5],
        matrix_sum(grad_expand_weight),
        sums[6],
        matrix_sum(grad_reduce_weight),
        sums[7],
    )


def solution(mesh):
    act = P("img", "band", None)
    row = P("img")
    mat = P("img", None)
    return jax.shard_map(
        local,
        mesh=mesh,
        in_specs=(act, P("img", "band"), P("img", None)) + (P(),) * 13 + (act,),
        out_specs=(act, act, row, row, mat, row, P(), mat, row, row, row, mat, row, mat, row),
        check_vma=False,
    )
```

time: 1040 us -> 658 us (0.63)
  waiting for transfers between devices: 519 us -> 220 us
  local copies, waits for them, and re-layouts: 178 us -> 95.8 us
  starting transfers between devices: 0.95 us -> 22.4 us
  blocking collectives: 91.4 us -> 72.8 us
  other arithmetic: 84.9 us -> 99.8 us
  matrix products: 136 us -> 125 us
    reduce_scatter x4 -> x5, waiting for transfers between devices: 428 us -> 147 us  [the longest x4 91.9 us: matrix_sum(): low = lax.psum_scatter(low, 'band', scatter_dimension=1, tiled=True)]
    all_gather x2 -> x0, waiting for transfers between devices: 61 us -> none  [the longest x1 34.6 us: local(): lax.all_gather(key_rot, 'band', axis=1, tiled=True)]
    unnamed x135 -> x127, local copies, waits for them, and re-layouts: 116 us -> 57.3 us
    unnamed x11, waiting for transfers between devices: 16.6 us -> 72.2 us
    unnamed x1 -> x0, blocking collectives: 36.9 us -> none
    sub x0 -> x2, other arithmetic: none -> 28.8 us  [the longest x1 22.2 us: local(): expo = jnp.exp(masked - jnp.max(masked, -1, keepdims=True))]
    all_gather x1 -> x4, blocking collectives: 6.52 us -> 31.2 us  [matrix_sum(): low = lax.all_gather(low, 'band', axis=1, tiled=True)]
    all_to_all x0 -> x5, starting transfers between devices: none -> 21.4 us  [the longest x3 12.7 us: gather_image(): return lax.all_to_all(values, 'band', 0, 1, tiled=True)]
  transfers between devices with their start and end apart: 9 -> 13, of which waited for: 7 -> 7; matrix products, arithmetic and copies ran while one was open for 23% -> 38% of each run, Pallas kernels for 0% -> 0%
where the time goes in v1:
time: 658 us; the launch traced here: 652 us
  waiting for transfers between devices  220 us (33%)
  matrix products  125 us (19%)
  other arithmetic  99.8 us (15%)
  local copies, waits for them, and re-layouts  95.8 us (15%)
  blocking collectives  72.8 us (11%)
  starting transfers between devices  22.4 us (3%)
  between operations  15.3 us (2%)
    reduce_scatter x4, waiting for transfers between devices, matrix_sum(): low = lax.psum_scatter(low, 'band', scatter_dimension=1, tiled=True)  91.9 us
    unnamed x11, waiting for transfers between devices  72.2 us
    unnamed x127, local copies, waits for them, and re-layouts  57.3 us
    reduce_scatter x1, waiting for transfers between devices, matrix_sum(): low = lax.psum_scatter(low, 'img', scatter_dimension=0, tiled=True)  54.7 us
    psum x1, blocking collectives, local(): packed = lax.psum(jnp.concatenate(small), ('img', 'band'))  41.6 us
    all_gather x4, blocking collectives, matrix_sum(): low = lax.all_gather(low, 'band', axis=1, tiled=True)  31.2 us
    sub x1, other arithmetic, local(): expo = jnp.exp(masked - jnp.max(masked, -1, keepdims=True))  22.2 us
    unnamed x3, other arithmetic  16 us
  transfers between devices with their start and end apart: 13, of which 7 were waited for; matrix products, arithmetic and copies ran while one was open for 38% of the time, Pallas kernels for 0%

profile of v1, /device:TPU:0, one launch (start us, length us, event | category | flops | bytes accessed | tf_op | source)
XLA Modules:
  0.0 651.7 jit_solution(12072034389343736507)
XLA Ops:
  45.8 4.6 convolution_add_fusion
  50.3 6.5 copy.68
  59.3 4.8 subtract_convert_fusion.1
  65.4 7.4 %fusion.34 = f32[12,576,576]{1,2,0:T(8,128)} fusion(bf16[576,12,32]{0,2,1:T(8,128)(2,1)S(1)} %bitcast.128, bf16[576,12,32]{0,2,1:T(8,128)(2,1)S(1)} %bitcast.130, bf16[576,12,32]{0,2,1:T(8,128)(2,1)S(1)} %bitcast.126, bf16[576,12,32]{0,2,1:T(8,128)(2,1)S(1)} %bitcast.124), kind=kOutput, calls=%fused_computation.88 | convolution fusion | flops 513146880 | bytes 17694720 | tf_op jit(solution)/shard_map/iqhd,ikhd->ihqk/dot_general | solution.py:98
  72.7 22.2 %fusion.54 = (f32[12,576]{1,0:T(8,128)}, f32[12,576,576]{1,2,0:T(8,128)}) fusion(f32[12,576,576]{1,2,0:T(8,128)} %fusion.34, pred[576]{0:T(1024)(128)(4,1)} %broadcast_compare_fusion), kind=kOutput, calls=%fused_computation.138 | output fusion | flops 23888448 | bytes 31878720 | tf_op jit(solution)/shard_map/sub | solution.py:100
  94.9 8.4 %fusion.21 = bf16[12,64,576]{2,1,0:T(8,128)(2,1)S(1)} fusion(f32[1,576,3,12,64]{1,4,3,2,0:T(8,128)} %bitcast.122, f32[12,576,576]{1,2,0:T(8,128)} %get-tuple-element.113, f32[12,576]{1,0:T(8,128)} %get-tuple-element.112), kind=kOutput, calls=%fused_computation.63 | convolution fusion | flops 518012928 | bytes 19603456 | tf_op jit(solution)/shard_map/ihqk,ikhd->iqhd/dot_general | solution.py:103
  112.8 8.9 %multiply_convert_fusion.1 = (bf16[576,3072]{1,0:T(8,128)(2,1)}, f32[576,3072]{1,0:T(8,128)}) fusion(f32[3072]{0:T(1024)} %convert_element_type.313, bf16[768,3072]{1,0:T(8,128)(2,1)} %param.29, f32[576,768]{1,0:T(8,128)} %fusion.20, f32[768]{0:T(1024)} %convert_element_type.311, f32[768]{0:T(1024)} %convert_element_type.310, f32[576]{0:T(1024)S(1)} %add_rsqrt_fusion, ...), kind=kOutput, calls=%fused_computation.18 | convolution fusion | flops 2730737664 | bytes 17127936 | tf_op jit(solution)/shard_map/dot_general | solution.py:110
  123.2 9.2 %convert_reduce_fusion = (f32[3072]{0:T(1024)}, bf16[576,3072]{1,0:T(8,128)(2,1)S(1)}) fusion(f32[576,3072]{1,0:T(8,128)} %get-tuple-element.115, f32[3072]{0:T(1024)} %convert_element_type.313, bf16[576,768]{1,0:T(8,128)(2,1)S(1)} %fusion.19, bf16[3072,768]{1,0:T(8,128)(2,1)} %param.31), kind=kOutput, calls=%fused_computation.17 | convolution fusion | flops 2740909056 | bytes 16244736 | tf_op jit(solution)/shard_map/iqd,fd->iqf/dot_general | solution.py:123
  132.4 7.6 %multiply_reduce_fusion.1 = (f32[768]{0:T(1024)}, f32[576]{0:T(1024)S(1)}, f32[576]{0:T(1024)S(1)}, f32[768]{0:T(1024)}, f32[576,768]{1,0:T(8,128)S(1)}) fusion(f32[576,768]{1,0:T(8,128)S(1)} %copy-done.1, f32[576]{0:T(1024)S(1)} %copy-done.40, f32[576]{0:T(1024)S(1)} %copy-done.32, f32[768]{0:T(1024)S(1)} %copy-done.37, ...), kind=kOutput, calls=%fused_computation.46 | convolution fusion | flops 2721887744 | bytes 11814912 | tf_op jit(solution)/shard_map/iqf,df->iqd/dot_general | solution.py:127
  151.8 15.5 %multiply_reduce_fusion = (f32[12,576]{1,0:T(8,128)S(1)}, f32[12,576,576]{1,2,0:T(8,128)}) fusion(f32[12,576,576]{1,2,0:T(8,128)} %get-tuple-element.113, f32[12,576]{1,0:T(8,128)} %get-tuple-element.112, bf16[576,12,64]{0,2,1:T(8,128)(2,1)} %bitcast.144, f32[1,576,3,12,64]{1,4,3,2,0:T(8,128)} %bitcast.123), kind=kOutput, calls=%fused_computation.2 | convolution fusion | flops 521544960 | bytes 35654656 | tf_op jit(solution)/shard_map/iqhd,ikhd->ihqk/dot_general | solution.py:137
  167.3 12.5 %multiply_convert_fusion = bf16[12,576,576]{1,2,0:T(8,128)(2,1)S(1)} fusion(f32[12,576,576]{1,2,0:T(8,128)} %get-tuple-element.118, f32[12,576]{1,0:T(8,128)S(1)} %get-tuple-element.117, f32[12,576,576]{1,2,0:T(8,128)} %get-tuple-element.113, f32[12,576]{1,0:T(8,128)S(1)} %copy-done.27), kind=kLoop, calls=%fused_computation.1 | loop fusion | flops 15925248 | bytes 39868416 | tf_op jit(solution)/shard_map/convert_element_type | solution.py:139
  186.9 6.6 %multiply_subtract_fusion.1 = (bf16[1,576,12,32]{1,3,2,0:T(8,128)(2,1)S(1)}, bf16[1,576,12,32]{1,3,2,0:T(8,128)(2,1)S(1)}, bf16[1,576,12,32]{1,3,2,0:T(8,128)(2,1)S(1)}, bf16[1,576,12,32]{1,3,2,0:T(8,128)(2,1)S(1)}) fusion(f32[1,576,12,64]{1,3,2,0:T(8,128)} %multiply_bitcast_fusion.1, f32[12,32]{1,0:T(8,128)} %get-tuple-element.111, f32[576]{0:T(1024)S(1)} %copy-done.24, ...), kind=kLoop, calls=%fused_computation.78 | loop fusion | flops 4423680 | bytes 5316096 | tf_op jit(solution)/shard_map/sub | solution.py:27
  195.1 9.5 %fusion.24 = bf16[12,64,576]{2,1,0:T(8,128)(2,1)S(1)} fusion(bf16[576,12,64]{0,2,1:T(8,128)(2,1)S(1)} %bitcast.145, f32[12,576,576]{1,2,0:T(8,128)} %get-tuple-element.113, f32[12,576]{1,0:T(8,128)S(1)} %copy-done.28), kind=kOutput, calls=%fused_computation.64 | convolution fusion | flops 518012928 | bytes 17722368 | tf_op jit(solution)/shard_map/ihqk,iqhd->ikhd/dot_general | solution.py:136
  205.6 7.2 %convolution_convert_fusion = bf16[768,2304]{0,1:T(8,128)(2,1)} fusion(bf16[576,768]{0,1:T(8,128)(2,1)S(1)} %bitcast.146, bf16[576,768]{0,1:T(8,128)(2,1)S(1)} %bitcast.141, bf16[576,768]{0,1:T(8,128)(2,1)S(1)} %bitcast.138, f32[576,768]{1,0:T(8,128)S(1)} %copy-done.16, f32[768]{0:T(1024)S(1)} %copy-done.43, f32[768]{0:T(1024)S(1)} %copy-done.35), kind=kOutput, calls=%fused_computation.21 | convolution fusion | flops 2049490944 | bytes 7968768 | tf_op jit(solution)/shard_map/iqd,iqe->de/dot_general | solution.py:158
  213.0 8.3 %convolution_convert_fusion.1 = bf16[3072,768]{0,1:T(8,128)(2,1)} fusion(bf16[576,3072]{1,0:T(8,128)(2,1)} %get-tuple-element.114, bf16[576,768]{1,0:T(8,128)(2,1)} %copy-done.20), kind=kOutput, calls=%fused_computation.22 | convolution fusion | flops 2720268288 | bytes 9142272 | tf_op jit(solution)/shard_map/iqf,iqd->fd/dot_general | solution.py:121
  222.1 9.2 %convolution_convert_fusion.2 = bf16[768,3072]{1,0:T(8,128)(2,1)} fusion(bf16[576,3072]{1,0:T(8,128)(2,1)} %copy-done.50, f32[576,768]{1,0:T(8,128)} %fusion.20, f32[768]{0:T(1024)} %convert_element_type.311, f32[768]{0:T(1024)S(1)} %copy-done.38, f32[576]{0:T(1024)} %copy-done.39, f32[576]{0:T(1024)S(1)} %copy-done.33), kind=kOutput, calls=%fused_computation.23 | convolution fusion | flops 2722480128 | bytes 10037760 | tf_op jit(solution)/shard_map/iqd,iqf->df/dot_general | solution.py:125
  233.4 24.4 %reduce-scatter.15.cloned.1.call-done = bf16[768,576]{0,1:T(8,128)(2,1)} async-done(((bf16[768,2304]{0,1:T(8,128)(2,1)}), bf16[768,576]{0,1:T(8,128)(2,1)}) %reduce-scatter.15.cloned.1.call-update) | async-done | bytes 884752 | tf_op jit(solution)/shard_map/reduce_scatter | solution.py:33
  260.3 48.0 %reduce-scatter.23.cloned.1.call-done = bf16[3072,192]{0,1:T(8,128)(2,1)} async-done(((bf16[3072,768]{0,1:T(8,128)(2,1)}), bf16[3072,192]{0,1:T(8,128)(2,1)}) %reduce-scatter.23.cloned.1.call-update) | async-done | bytes 1179664 | tf_op jit(solution)/shard_map/reduce_scatter | solution.py:33
  310.8 6.8 %fusion.27 = bf16[1,576,768]{2,1,0:T(8,128)(2,1)S(1)} fusion(f32[576,768]{1,0:T(8,128)} %fusion.20, bf16[576,3072]{1,0:T(8,128)(2,1)} %get-tuple-element.114, bf16[3072,768]{1,0:T(8,128)(2,1)} %param.31, f32[768]{0:T(1024)S(1)} %convert_element_type.315, f32[576]{0:T(1024)S(1)} %convert_element_type.290), kind=kOutput, calls=%fused_computation.67 | convolution fusion | flops 2719678464 | bytes 10917120 | tf_op jit(solution)/shard_map/dot_general | solution.py:115
  320.8 8.0 %reduce.39 = bf16[576,768]{1,0:T(8,128)(2,1)} reduce(bf16[576,1,768]{2,1,0:T(2,128)(2,1)} %bitcast.134, bf16[]{:T(256)} %broadcast.353), dimensions={1}, to_apply=%bitcast.118.reduce_sub_computation | reduce | bytes 1769474
  336.8 6.8 %fusion.52 = (f32[768]{0:T(1024)S(1)}, f32[768]{0:T(1024)S(1)}, f32[576]{0:T(1024)S(1)}, f32[576]{0:T(1024)S(1)}, f32[576,768]{1,0:T(8,128)}) fusion(f32[576]{0:T(1024)S(1)} %copy-done.30, f32[576]{0:T(1024)S(1)} %copy-done.23, bf16[4,144,768]{2,1,0:T(8,128)(2,1)} %all-to-all-done.1, f32[576,768]{1,0:T(8,128)} %copy-done.15, ...), kind=kOutput, calls=%fused_computation.136 | convolution fusion | flops 2050815488 | bytes 10635264 | tf_op jit(solution)/shard_map/iqe,de->iqd/dot_general | solution.py:160
  348.6 19.5 %reduce-scatter.19.cloned.1.call-done = bf16[768,768]{1,0:T(8,128)(2,1)} async-done(((bf16[768,3072]{1,0:T(8,128)(2,1)}), bf16[768,768]{1,0:T(8,128)(2,1)}) %reduce-scatter.19.cloned.1.call-update) | async-done | bytes 1179664 | tf_op jit(solution)/shard_map/reduce_scatter | solution.py:33
  376.2 7.9 %reduce.40 = bf16[576,768]{1,0:T(8,128)(2,1)} reduce(bf16[576,1,768]{2,1,0:T(2,128)(2,1)} %bitcast.135, bf16[]{:T(256)} %broadcast.353), dimensions={1}, to_apply=%bitcast.117.reduce_sub_computation | reduce | bytes 1769474
  394.0 4.5 all-to-all-start.4
  404.8 41.6 %psum.7 = f32[10752]{0:T(1024)} all-reduce(f32[10752]{0:T(1024)} %constant_dynamic-update-slice_fusion), channel_id=1, replica_groups=mesh['img'=8,'band'=4] {'img','band'}, use_global_device_ids=true, to_apply=%region_21.22 | all-reduce | flops 10752 | bytes 86016 | tf_op jit(solution)/shard_map/psum | solution.py:177
  472.2 7.9 %all_gather.13 = bf16[96,768]{0,1:T(8,128)(2,1)} all-gather(bf16[96,192]{0,1:T(8,128)(2,1)} %copy.89), channel_id=1, replica_groups=mesh['img'=8,'band'=4] {'band'}, dimensions={1}, use_global_device_ids=true | all-gather | bytes 184320 | tf_op jit(solution)/shard_map/all_gather | solution.py:35
  481.9 18.5 %reduce-scatter.25.cloned.1.call-done = bf16[96,576]{1,0:T(8,128)(2,1)} async-done(((bf16[768,576]{1,0:T(8,128)(2,1)}), bf16[96,576]{1,0:T(8,128)(2,1)}) %reduce-scatter.25.cloned.1.call-update) | async-done | bytes 110608
  503.8 7.2 %all-gather = bf16[4,576,96]{1,2,0:T(8,128)(2,1)S(1)} all-gather(bf16[1,576,96]{1,2,0:T(8,128)(2,1)} %copy.77), channel_id=1, replica_groups=mesh['img'=8,'band'=4] {'band'}, dimensions={0}, use_global_device_ids=true | all-gather | bytes 552960 | tf_op jit(solution)/shard_map/all_gather | solution.py:35
  514.9 53.6 %reduce-scatter.29.cloned.1.call-done = bf16[384,192]{1,0:T(8,128)(2,1)} async-done(((bf16[3072,192]{1,0:T(8,128)(2,1)}), bf16[384,192]{1,0:T(8,128)(2,1)}) %reduce-scatter.29.cloned.1.call-update) | async-done | bytes 147472
  570.2 8.4 %all_gather.15 = bf16[384,768]{0,1:T(8,128)(2,1)} all-gather(bf16[384,192]{0,1:T(8,128)(2,1)} %copy.91), channel_id=1, replica_groups=mesh['img'=8,'band'=4] {'band'}, dimensions={1}, use_global_device_ids=true | all-gather | bytes 737280 | tf_op jit(solution)/shard_map/all_gather | solution.py:35
  580.8 54.7 %reduce-scatter.21.cloned.1.call-done = bf16[96,768]{1,0:T(8,128)(2,1)} async-done(((bf16[768,768]{1,0:T(8,128)(2,1)}), bf16[96,768]{1,0:T(8,128)(2,1)}) %reduce-scatter.21.cloned.1.call-update) | async-done | bytes 147472 | tf_op jit(solution)/shard_map/reduce_scatter | solution.py:34
  635.5 7.7 %all_gather.14 = bf16[96,3072]{1,0:T(8,128)(2,1)S(1)} all-gather(bf16[96,768]{1,0:T(8,128)(2,1)} %reduce-scatter.21.cloned.1.call-done), channel_id=1, replica_groups=mesh['img'=8,'band'=4] {'band'}, dimensions={1}, use_global_device_ids=true | all-gather | bytes 737280 | tf_op jit(solution)/shard_map/all_gather | solution.py:35
  (227 shorter events, 162.6 us)
Async XLA Ops:
  7.2 38.6 %copy-start = (bf16[768,2304]{1,0:T(8,128)(2,1)S(1)}, bf16[768,2304]{1,0:T(8,128)(2,1)}, u32[]{:S(2)}) copy-start(bf16[768,2304]{1,0:T(8,128)(2,1)} %param.22) | copy-start | bytes 10616836
  8.6 8.0 %all-to-all-start = ((s32[4,1,144]{2,1,0:T(1,128)}), s32[4,1,144]{2,1,0:T(1,128)S(1)}, u32[]{:S(2)}, u32[]{:S(2)}) async-start(s32[4,1,144]{2,1,0:T(1,128)} %all_to_all.17), calls=%async_computation | async-start | bytes 8192 | tf_op jit(solution)/shard_map/all_to_all | solution.py:68
  16.7 17.0 %all-to-all-start.1 = ((bf16[4,144,768]{2,1,0:T(8,128)(2,1)}), bf16[4,144,768]{2,1,0:T(8,128)(2,1)}, u32[]{:S(2)}, u32[]{:S(2)}) async-start(bf16[4,144,768]{2,1,0:T(8,128)(2,1)} %param.17), calls=%async_computation.1 | async-start | bytes 1769472 | tf_op jit(solution)/shard_map/all_to_all | solution.py:68
  33.7 88.0 %all-to-all-start.3 = ((bf16[4,144,768]{2,1,0:T(8,128)(2,1)}), bf16[4,144,768]{2,1,0:T(8,128)(2,1)}, u32[]{:S(2)}, u32[]{:S(2)}) async-start(bf16[4,144,768]{2,1,0:T(8,128)(2,1)} %param.33), calls=%async_computation.3 | async-start | bytes 1769472 | tf_op jit(solution)/shard_map/all_to_all | solution.py:68
  37.9 193.4 %reduce-scatter.17.cloned.1.call-start = ((), (), s32[]{:S(2)}) async-start(), calls=%async_computation.14 | async-start | bytes 1474560 | tf_op jit(solution)/shard_map/reduce_scatter | solution.py:33
  94.9 9.3 %copy-start.44 = (f32[768]{0:T(1024)S(1)}, f32[768]{0:T(1024)}, u32[]{:S(2)}) copy-start(f32[768]{0:T(1024)} %convert_element_type.309) | copy-start | bytes 9220
  94.9 9.3 %copy-start.47 = (bf16[768,768]{1,0:T(8,128)(2,1)S(1)}, bf16[768,768]{1,0:T(8,128)(2,1)}, u32[]{:S(2)}) copy-start(bf16[768,768]{1,0:T(8,128)(2,1)} %param.25) | copy-start | bytes 3538948
  123.1 9.2 %copy-start.20 = (bf16[576,768]{1,0:T(8,128)(2,1)}, bf16[576,768]{1,0:T(8,128)(2,1)S(1)}, u32[]{:S(2)}) copy-start(bf16[576,768]{1,0:T(8,128)(2,1)S(1)} %fusion.19) | copy-start | bytes 2654212
  123.1 9.2 %copy-start.1 = (f32[576,768]{1,0:T(8,128)S(1)}, f32[576,768]{1,0:T(8,128)}, u32[]{:S(2)}) copy-start(f32[576,768]{1,0:T(8,128)} %fusion.20) | copy-start | bytes 5308420
  151.8 15.5 %copy-start.27 = (f32[12,576]{1,0:T(8,128)S(1)}, f32[12,576]{1,0:T(8,128)}, u32[]{:S(2)}) copy-start(f32[12,576]{1,0:T(8,128)} %get-tuple-element.112) | copy-start | bytes 82948
  167.3 12.5 %copy-start.3 = (bf16[1,576,12,32]{1,3,2,0:T(8,128)(2,1)S(1)}, bf16[1,576,12,32]{1,3,2,0:T(8,128)(2,1)}, u32[]{:S(2)}) copy-start(bf16[1,576,12,32]{1,3,2,0:T(8,128)(2,1)} %copy-done.2) | copy-start | bytes 1327108
  167.3 12.6 %copy-start.5 = (bf16[1,576,12,32]{1,3,2,0:T(8,128)(2,1)S(1)}, bf16[1,576,12,32]{1,3,2,0:T(8,128)(2,1)}, u32[]{:S(2)}) copy-start(bf16[1,576,12,32]{1,3,2,0:T(8,128)(2,1)} %copy-done.4) | copy-start | bytes 1327108
  186.9 70.9 %reduce-scatter.15.cloned.1.call-start = ((), (), s32[]{:S(2)}) async-start(), calls=%async_computation.13 | async-start | bytes 4423680 | tf_op jit(solution)/shard_map/reduce_scatter | solution.py:33
  193.6 11.0 %copy-start.11 = (bf16[1,576,12,64]{1,3,2,0:T(8,128)(2,1)}, bf16[1,576,12,64]{1,3,2,0:T(8,128)(2,1)S(1)}, u32[]{:S(2)}) copy-start(bf16[1,576,12,64]{1,3,2,0:T(8,128)(2,1)S(1)} %maximum_convert_fusion) | copy-start | bytes 2654212
  195.1 9.5 %copy-start.13 = (bf16[1,576,12,64]{1,3,2,0:T(8,128)(2,1)}, bf16[1,576,12,64]{1,3,2,0:T(8,128)(2,1)S(1)}, u32[]{:S(2)}) copy-start(bf16[1,576,12,64]{1,3,2,0:T(8,128)(2,1)S(1)} %maximum_convert_fusion.1) | copy-start | bytes 2654212
  195.1 10.5 %copy-start.16 = (f32[576,768]{1,0:T(8,128)S(1)}, f32[576,768]{1,0:T(8,128)}, u32[]{:S(2)}) copy-start(f32[576,768]{1,0:T(8,128)} %copy-done.15) | copy-start | bytes 5308420
  195.1 10.5 %copy-start.35 = (f32[768]{0:T(1024)S(1)}, f32[768]{0:T(1024)}, u32[]{:S(2)}) copy-start(f32[768]{0:T(1024)} %convert_element_type.296) | copy-start | bytes 9220
  195.1 10.4 %copy-start.43 = (f32[768]{0:T(1024)S(1)}, f32[768]{0:T(1024)}, u32[]{:S(2)}) copy-start(f32[768]{0:T(1024)} %convert_element_type.297) | copy-start | bytes 9220
  212.8 95.5 %reduce-scatter.23.cloned.1.call-start = ((), (), s32[]{:S(2)}) async-start(), calls=%async_computation.17 | async-start | bytes 5898240 | tf_op jit(solution)/shard_map/reduce_scatter | solution.py:33
  221.4 146.7 %reduce-scatter.19.cloned.1.call-start = ((), (), s32[]{:S(2)}) async-start(), calls=%async_computation.15 | async-start | bytes 5898240 | tf_op jit(solution)/shard_map/reduce_scatter | solution.py:33
  231.3 29.0 %copy-start.46 = (bf16[768]{0:T(1024)(128)(2,1)S(1)}, bf16[768]{0:T(1024)(128)(2,1)}, u32[]{:S(2)}) copy-start(bf16[768]{0:T(1024)(128)(2,1)} %param.32) | copy-start | bytes 4612
  231.3 239.4 %reduce-scatter.27.cloned.1.call-start = ((), (), s32[]{:S(2)}) async-start(), calls=%async_computation.19 | async-start | bytes 442368
  233.3 267.1 %reduce-scatter.25.cloned.1.call-start = ((), (), s32[]{:S(2)}) async-start(), calls=%async_computation.18 | async-start | bytes 1105920
  260.0 308.4 %reduce-scatter.29.cloned.1.call-start = ((), (), s32[]{:S(2)}) async-start(), calls=%async_computation.20 | async-start | bytes 1769472
  332.3 61.7 %all-to-all-start.2 = ((bf16[4,2,55296]{2,1,0:T(2,128)(2,1)}), bf16[4,2,55296]{2,1,0:T(2,128)(2,1)}, u32[]{:S(2)}, u32[]{:S(2)}) async-start(bf16[4,2,55296]{2,1,0:T(2,128)(2,1)} %reshape.788), calls=%async_computation.2 | async-start | bytes 1769472 | tf_op jit(solution)/shard_map/all_to_all | solution.py:71
  336.5 299.0 %reduce-scatter.21.cloned.1.call-start = ((), (), s32[]{:S(2)}) async-start(), calls=%async_computation.16 | async-start | bytes 1327104 | tf_op jit(solution)/shard_map/reduce_scatter | solution.py:34
  336.8 9.4 %copy-start.12 = (bf16[1,576,12,64]{1,3,2,0:T(8,128)(2,1)S(1)}, bf16[1,576,12,64]{1,3,2,0:T(8,128)(2,1)}, u32[]{:S(2)}) copy-start(bf16[1,576,12,64]{1,3,2,0:T(8,128)(2,1)} %copy-done.11) | copy-start | bytes 2654212
  336.8 9.4 %copy-start.14 = (bf16[1,576,12,64]{1,3,2,0:T(8,128)(2,1)S(1)}, bf16[1,576,12,64]{1,3,2,0:T(8,128)(2,1)}, u32[]{:S(2)}) copy-start(bf16[1,576,12,64]{1,3,2,0:T(8,128)(2,1)} %copy-done.13) | copy-start | bytes 2654212
  336.8 9.4 %copy-start.19 = (bf16[12,64,576]{2,1,0:T(8,128)(2,1)S(1)}, bf16[12,64,576]{2,1,0:T(8,128)(2,1)}, u32[]{:S(2)}) copy-start(bf16[12,64,576]{2,1,0:T(8,128)(2,1)} %copy-done.18) | copy-start | bytes 2654212
  376.2 12.6 %copy-start.45 = (f32[768]{0:T(1024)S(1)}, f32[768]{0:T(1024)}, u32[]{:S(2)}) copy-start(f32[768]{0:T(1024)} %get-tuple-element.80) | copy-start | bytes 9220
  376.2 13.9 %copy-start.26 = (f32[576]{0:T(1024)S(1)}, f32[576]{0:T(1024)}, u32[]{:S(2)}) copy-start(f32[576]{0:T(1024)} %get-tuple-element.123) | copy-start | bytes 6916
  394.0 70.3 %all-to-all-start.4 = ((bf16[4,2,55296]{2,1,0:T(2,128)(2,1)}), bf16[4,2,55296]{2,1,0:T(2,128)(2,1)}, u32[]{:S(2)}, u32[]{:S(2)}) async-start(bf16[4,2,55296]{2,1,0:T(2,128)(2,1)} %reshape.790), calls=%async_computation.4 | async-start | bytes 1769472 | tf_op jit(solution)/shard_map/all_to_all | solution.py:71
  (32 other events, 102.0 us)
Sparse Core Ops, SparseCore 0:
  187.0 27.7 reduce-scatter.16
  217.4 40.3 reduce-scatter.14
  260.3 47.9 reduce-scatter.22
  310.7 57.2 reduce-scatter.18
  371.1 62.2 reduce-scatter.26
  437.2 63.1 reduce-scatter.24
  503.8 64.5 reduce-scatter.28
  571.9 63.6 reduce-scatter.20
